TPU v7x, 32 devices: a whole 2x2x4 slice. The times are simulated.
32 devices in a mesh: ckpt: 4 (over z), shard: 8 (over y, x, core).
Axes of the slice: x: 2, y: 2, z: 4, core: 2. Of those that a mesh axis runs over, the one named last changes fastest.
Arguments:
- task_vectors: bfloat16 [4, 4096, 16384], P('ckpt', 'shard'), may hold values from -0.125 to 0.125, as said below
- thresholds: float32 [4], replicated, may hold values from 0.009 to 0.062, as said below
- base_weight: float32 [4096, 16384], P('ckpt', 'shard'), may hold values from -0.3 to 0.3
Outputs:
- merged: float32 [4096, 16384], P('ckpt', 'shard')
Inputs may be any that keep to these rules, and one draw needn't show every extreme that they name: `task_vectors`: every entry is a whole multiple of 2^-14. `thresholds`: every threshold is an odd multiple of 2^-15.
All inputs are finite; a program needn't handle non-finite values.
Results may differ from a plain program's by a relative error of at most 0.0003.
Values may be sent and summed in bfloat16 or wider, within the bound.
A program may use at most 128 MiB of HBM per device.

v0:
```python
import jax
import jax.numpy as jnp
from jax import lax
from jax.sharding import PartitionSpec as P


def local_mean(all_tasks, limits):
    values = all_tasks.astype(jnp.float32)
    trimmed = jnp.where(jnp.abs(values) > limits[:, None, None], values, jnp.float32(0.0))
    signed_total = jnp.sum(trimmed, axis=0)
    agreeing = jnp.logical_or(
        jnp.logical_and(signed_total[None] > 0, trimmed > 0),
        jnp.logical_and(signed_total[None] < 0, trimmed < 0),
    )
    kept_sum = jnp.sum(jnp.where(agreeing, trimmed, jnp.float32(0.0)), axis=0)
    agree_count = jnp.sum(agreeing.astype(jnp.float32), axis=0)
    return jnp.where(agree_count > 0, kept_sum / jnp.maximum(agree_count, 1.0), jnp.float32(0.0))


def local(task_vectors, thresholds, base_weight):
    ckpt_count = lax.axis_size("ckpt")
    shard_count = lax.axis_size("shard")
    all_tasks = lax.all_to_all(task_vectors, "ckpt", split_axis=1, concat_axis=0, tiled=True)
    mean_part = local_mean(all_tasks, thresholds)
    block_rows = mean_part.shape[0]
    by_columns = lax.all_to_all(mean_part, "shard", split_axis=1, concat_axis=0, tiled=True)
    col_width = by_columns.shape[1]
    by_rows = lax.all_to_all(by_columns, "ckpt", split_axis=0, concat_axis=0, tiled=True)
    group_size = shard_count // ckpt_count
    disjoint = by_rows.reshape(ckpt_count, group_size, block_rows, col_width)
    disjoint = disjoint.transpose(1, 0, 2, 3).reshape(
        group_size * ckpt_count * block_rows, col_width
    )
    return base_weight + disjoint


def solution(mesh):
    placed = (P("ckpt", "shard", None), P(), P("ckpt", "shard"))
    return jax.shard_map(
        local, mesh=mesh, in_specs=placed, out_specs=P("ckpt", "shard"), check_vma=False
    )
```

profile of v0, /device:TPU:0, one launch (start us, length us, event | category | flops | bytes accessed | tf_op | source)
XLA Modules:
  0.0 955.8 jit_solution(856141177414765462)
XLA Ops:
  0.0 29.1 %copy.18 = bf16[1,512,16384]{2,0,1:T(2,128)(2,1)} copy(bf16[1,512,16384]{2,1,0:T(8,128)(2,1)} %param.3) | data formatting | bytes 33554432 | tf_op args[0]
  29.1 0.5 broadcast.94
  29.6 99.6 %reduce = bf16[512,16384]{1,0:T(8,128)(2,1)} reduce(bf16[512,1,16384]{2,1,0:T(2,128)(2,1)} %bitcast.16, bf16[]{:T(256)} %broadcast.94), dimensions={1}, to_apply=%bitcast.13.reduce_sub_computation | reduce | bytes 33554432
  129.3 17.4 %reshape.60 = bf16[4,2,1048576]{2,1,0:T(2,128)(2,1)} reshape(bf16[512,16384]{1,0:T(8,128)(2,1)} %reduce) | data formatting | bytes 33554432
  146.6 375.8 %all_to_all.31 = bf16[4,2,1048576]{2,1,0:T(2,128)(2,1)} all-to-all(bf16[4,2,1048576]{2,1,0:T(2,128)(2,1)} %reshape.60), channel_id=1, replica_groups=mesh['ckpt'=4,'shard'=8] {'ckpt'}, dimensions={0} | all-to-all | bytes 33554432 | tf_op jit(solution)/shard_map/all_to_all | solution.py:23
  522.4 35.6 %reshape.61 = bf16[512,1,16384]{2,1,0:T(2,128)(2,1)} reshape(bf16[4,2,1048576]{2,1,0:T(2,128)(2,1)} %all_to_all.31) | data formatting | bytes 33554432
  558.0 0.0 copy-start
  558.1 28.2 %copy.13 = bf16[1,512,16384]{2,1,0:T(8,128)(2,1)S(1)} copy(bf16[1,512,16384]{2,0,1:T(2,128)(2,1)} %bitcast.17) | data formatting | bytes 33554432 | tf_op jit(solution)/shard_map/all_to_all | solution.py:23
  586.3 0.0 copy-done
  586.3 13.3 %fusion.3 = f32[128,16384]{1,0:T(8,128)S(1)} fusion(bf16[4,128,16384]{2,1,0:T(8,128)(2,1)S(1)} %bitcast.14, f32[4]{0:T(128)S(1)} %copy-done), kind=kLoop, calls=%fused_computation.5 | loop fusion | flops 39845888 | bytes 25165840 | tf_op jit(solution)/shard_map/reduce_sum | solution.py:10
  599.6 3.8 broadcast_compare_fusion.1
  603.4 25.8 %convert_reduce_fusion = (f32[128,16384]{1,0:T(8,128)S(1)}, f32[128,16384]{1,0:T(8,128)}) fusion(f32[4]{0:T(128)S(1)} %copy-done, bf16[4,128,16384]{2,1,0:T(8,128)(2,1)S(1)} %bitcast.15, pred[128,16384]{1,0:T(8,128)(4,1)} %get-tuple-element.8, pred[128,16384]{1,0:T(8,128)(4,1)} %get-tuple-element.7), kind=kLoop, calls=%fused_computation.8 | loop fusion | flops 104857600 | bytes 37748752 | tf_op jit(solution)/shard_map/reduce_sum | solution.py:16
  629.1 6.3 divide_select_fusion
  635.4 9.0 copy.14
  644.4 99.7 %all_to_all.32 = f32[128,8,2048]{0,2,1:T(8,128)} all-to-all(f32[128,8,2048]{0,2,1:T(8,128)} %bitcast.18), channel_id=1, replica_groups=mesh['ckpt'=4,'shard'=8] {'shard'}, dimensions={1} | all-to-all | bytes 16777216 | tf_op jit(solution)/shard_map/all_to_all | solution.py:26
  744.1 9.1 copy.15
  753.3 186.9 %all_to_all.33 = f32[4,256,2048]{2,1,0:T(8,128)S(1)} all-to-all(f32[4,256,2048]{2,1,0:T(8,128)} %bitcast.20), channel_id=1, replica_groups=mesh['ckpt'=4,'shard'=8] {'ckpt'}, dimensions={0} | all-to-all | bytes 16777216 | tf_op jit(solution)/shard_map/all_to_all | solution.py:28
  940.1 3.8 copy.16
  943.9 11.9 %bitcast_add_fusion = f32[1024,2048]{1,0:T(8,128)} fusion(f32[1024,2048]{1,0:T(8,128)} %param.5, f32[2,4,128,2048]{3,2,1,0:T(8,128)} %copy.16), kind=kLoop, calls=%fused_computation.12 | loop fusion | flops 2097152 | bytes 25165824 | tf_op jit(solution)/shard_map/add | solution.py:34
Async XLA Ops:
  558.0 28.3 %copy-start = (f32[4]{0:T(128)S(1)}, f32[4]{0:T(128)}, u32[]{:S(2)}) copy-start(f32[4]{0:T(128)} %param.4) | copy-start | bytes 52
where the time goes:
time: 957 us; the launch traced here: 956 us
  blocking collectives  662 us (69%)
  other arithmetic  161 us (17%)
  local copies, waits for them, and re-layouts  133 us (14%)
    all_to_all x1, blocking collectives, local(): lax.all_to_all(task_vectors, 'ckpt', split_axis=1, concat_axis=0, tiled=T...  376 us
    all_to_all x1, blocking collectives, local(): lax.all_to_all(by_columns, 'ckpt', split_axis=0, concat_axis=0, tiled=True)  187 us
    all_to_all x1, blocking collectives, local(): lax.all_to_all(mean_part, 'shard', split_axis=1, concat_axis=0, tiled=True)  99.7 us
    unnamed x1, other arithmetic  99.6 us
    unnamed x6, local copies, waits for them, and re-layouts  82.6 us
    all_to_all x1, local copies, waits for them, and re-layouts, local(): lax.all_to_all(task_vectors, 'ckpt', split_axis=1, concat_axis=0, tiled=T...  28.2 us
    reduce_sum x1, other arithmetic, local_mean(): agree_count = jnp.sum(agreeing.astype(jnp.float32), axis=0)  25.8 us

commit v1 on v0

--- a/solution.py
+++ b/solution.py
@@ -23,7 +23,15 @@
     all_tasks = lax.all_to_all(task_vectors, "ckpt", split_axis=1, concat_axis=0, tiled=True)
     mean_part = local_mean(all_tasks, thresholds)
     block_rows = mean_part.shape[0]
-    by_columns = lax.all_to_all(mean_part, "shard", split_axis=1, concat_axis=0, tiled=True)
+    by_columns = jnp.concatenate(
+        lax.all_to_all(
+            jnp.stack(jnp.split(mean_part, lax.axis_size("shard"), axis=1), axis=0),
+            concat_axis=0,
+            split_axis=0,
+            axis_name="shard",
+        ),
+        axis=0,
+    )
     col_width = by_columns.shape[1]
     by_rows = lax.all_to_all(by_columns, "ckpt", split_axis=0, concat_axis=0, tiled=True)
     group_size = shard_count // ckpt_count

time: 957 us -> 933 us (0.975)
  local copies, waits for them, and re-layouts: 133 us -> 115 us
    unnamed x6 -> x13, local copies, waits for them, and re-layouts: 82.6 us -> 83.2 us
where the time goes in v1:
time: 933 us
  blocking collectives  659 us (71%)
  other arithmetic  158 us (17%)
  local copies, waits for them, and re-layouts  115 us (12%)
    all_to_all x1, blocking collectives, local(): lax.all_to_all(task_vectors, 'ckpt', split_axis=1, concat_axis=0, tiled=T...  376 us
    all_to_all x1, blocking collectives, local(): lax.all_to_all(by_columns, 'ckpt', split_axis=0, concat_axis=0, tiled=True)  185 us
    unnamed x1, other arithmetic  99.6 us
    all_to_all x1, blocking collectives, local(): lax.all_to_all(jnp.stack(jnp.split(mean_part, lax.axis_size('shard'), axi...  97.5 us
    unnamed x13, local copies, waits for them, and re-layouts  83.2 us
    all_to_all x1, local copies, waits for them, and re-layouts, local(): lax.all_to_all(task_vectors, 'ckpt', split_axis=1, concat_axis=0, tiled=T...  28.2 us
    reduce_sum x1, other arithmetic, local_mean(): agree_count = jnp.sum(agreeing.astype(jnp.float32), axis=0)  25.8 us

profile of v1, /device:TPU:0, one launch (start us, length us, event | category | flops | bytes accessed | tf_op | source)
XLA Modules:
  0.0 932.6 jit_solution(4184166912658508664)
XLA Ops:
  0.0 29.1 %copy.11 = bf16[1,512,16384]{2,0,1:T(2,128)(2,1)} copy(bf16[1,512,16384]{2,1,0:T(8,128)(2,1)} %param.3) | data formatting | bytes 33554432 | tf_op args[0]
  29.1 0.5 broadcast.85
  29.6 99.6 %reduce = bf16[512,16384]{1,0:T(8,128)(2,1)} reduce(bf16[512,1,16384]{2,1,0:T(2,128)(2,1)} %bitcast.46, bf16[]{:T(256)} %broadcast.85), dimensions={1}, to_apply=%bitcast.43.reduce_sub_computation | reduce | bytes 33554432
  129.3 17.4 %reshape.49 = bf16[4,2,1048576]{2,1,0:T(2,128)(2,1)} reshape(bf16[512,16384]{1,0:T(8,128)(2,1)} %reduce) | data formatting | bytes 33554432
  146.6 375.8 %all_to_all.23 = bf16[4,2,1048576]{2,1,0:T(2,128)(2,1)} all-to-all(bf16[4,2,1048576]{2,1,0:T(2,128)(2,1)} %reshape.49), channel_id=1, replica_groups=mesh['ckpt'=4,'shard'=8] {'ckpt'}, dimensions={0} | all-to-all | bytes 33554432 | tf_op jit(solution)/shard_map/all_to_all | solution.py:23
  522.4 35.6 %reshape.50 = bf16[512,1,16384]{2,1,0:T(2,128)(2,1)} reshape(bf16[4,2,1048576]{2,1,0:T(2,128)(2,1)} %all_to_all.23) | data formatting | bytes 33554432
  558.0 0.0 copy-start
  558.1 28.2 %copy.8 = bf16[1,512,16384]{2,1,0:T(8,128)(2,1)S(1)} copy(bf16[1,512,16384]{2,0,1:T(2,128)(2,1)} %bitcast.47) | data formatting | bytes 33554432 | tf_op jit(solution)/shard_map/all_to_all | solution.py:23
  586.3 0.0 copy-done
  586.3 13.3 %fusion.3 = f32[128,16384]{1,0:T(8,128)S(1)} fusion(bf16[4,128,16384]{2,1,0:T(8,128)(2,1)S(1)} %bitcast.44, f32[4]{0:T(128)S(1)} %copy-done), kind=kLoop, calls=%fused_computation.5 | loop fusion | flops 39845888 | bytes 25165840 | tf_op jit(solution)/shard_map/reduce_sum | solution.py:10
  599.6 3.8 broadcast_compare_fusion.1
  603.4 25.8 %convert_reduce_fusion = (f32[128,16384]{1,0:T(8,128)S(1)}, f32[128,16384]{1,0:T(8,128)}) fusion(f32[4]{0:T(128)S(1)} %copy-done, bf16[4,128,16384]{2,1,0:T(8,128)(2,1)S(1)} %bitcast.45, pred[128,16384]{1,0:T(8,128)(4,1)} %get-tuple-element.8, pred[128,16384]{1,0:T(8,128)(4,1)} %get-tuple-element.7), kind=kLoop, calls=%fused_computation.8 | loop fusion | flops 104857600 | bytes 37748752 | tf_op jit(solution)/shard_map/reduce_sum | solution.py:16
  629.1 4.2 divide_select_fusion
  633.3 0.1 fusion.16
  633.4 0.1 fusion.15
  633.5 0.1 fusion.14
  633.6 0.1 fusion.13
  633.6 0.1 fusion.12
  633.7 0.1 fusion.11
  633.8 0.1 fusion.10
  633.9 0.1 fusion.9
  634.0 97.5 %all_to_all.24 = f32[8,128,2048]{2,1,0:T(8,128)S(1)} all-to-all(f32[8,128,2048]{2,1,0:T(8,128)S(1)} %fusion.9), channel_id=1, replica_groups=mesh['ckpt'=4,'shard'=8] {'shard'}, dimensions={0} | all-to-all | bytes 16777216 | tf_op jit(solution)/shard_map/all_to_all | solution.py:27
  731.5 185.5 %all_to_all.25 = f32[4,256,2048]{2,1,0:T(8,128)S(1)} all-to-all(f32[4,256,2048]{2,1,0:T(8,128)S(1)} %bitcast.48), channel_id=1, replica_groups=mesh['ckpt'=4,'shard'=8] {'ckpt'}, dimensions={0} | all-to-all | bytes 16777216 | tf_op jit(solution)/shard_map/all_to_all | solution.py:36
  917.0 3.8 copy.9
  920.8 11.9 %bitcast_add_fusion = f32[1024,2048]{1,0:T(8,128)} fusion(f32[1024,2048]{1,0:T(8,128)} %param.5, f32[2,4,128,2048]{3,2,1,0:T(8,128)} %copy.9), kind=kLoop, calls=%fused_computation.12 | loop fusion | flops 2097152 | bytes 25165824 | tf_op jit(solution)/shard_map/add | solution.py:42
Async XLA Ops:
  558.0 28.3 %copy-start = (f32[4]{0:T(128)S(1)}, f32[4]{0:T(128)}, u32[]{:S(2)}) copy-start(f32[4]{0:T(128)} %param.4) | copy-start | bytes 52
